TPU v7x, 256 devices: a whole 4x4x8 slice. The times are simulated.
256 devices in a mesh: group: 8 (over x, core), member: 32 (over y, z).
Axes of the slice: x: 4, y: 4, z: 8, core: 2. Of those that a mesh axis runs over, the one named last changes fastest.
Arguments:
- q_rows: bfloat16 [65536, 8192], P(('group', 'member')), may hold values from -36 to 36
- own_kv: bfloat16 [65536, 1024], P(('group', 'member')), may hold values from -6 to 6
- cache: bfloat16 [1024, 64, 1024], P(('group', 'member')), may hold values from -6 to 6
- recomp_hidden: bfloat16 [512, 8, 16, 4096], P(('group', 'member')), may hold values from -6 to 6
- w_kv: bfloat16 [4096, 1024], P('member', 'group'), may hold values from -0.09375 to 0.09375
- retrieval: int32 [512, 8], P(('group', 'member')), may hold values from 0 to 127, as said below
- positions: int32 [512, 8, 16], P(('group', 'member')), may hold values from 0 to 63, as said below
Outputs:
- attn_out: bfloat16 [65536, 8192], P(('group', 'member'))
Inputs may be any that keep to these rules, and one draw needn't show every extreme that they name: `retrieval`: the 8 passages of one query are different. Passage i of a group's corpus is held by the device of member index i // 4 in that group. The queries of one device name at most 1 passages held by any one device, and this bound is reached. The 16 positions of one retrieved passage are different.
All inputs are finite; a program needn't handle non-finite values.
Results may differ from a plain program's by a relative error of at most 0.0054.
Values may be sent and summed in bfloat16 or wider, within the bound.
A program may use at most 128 MiB of HBM per device.

v0:
```python
import jax
import jax.numpy as jnp
from jax import lax
from jax.sharding import PartitionSpec as P

D = 4096
HQ = 64
KVH = 4
HD = 128
TOPP = 8
QLEN = 128
PLEN = 64
RECOMP = 16
EPSILON = 1e-06


def local(q_rows, own_kv, cache, recomp_hidden, w_kv, retrieval, positions):
    query_count = retrieval.shape[0]
    requests = query_count * TOPP
    kv_width = 2 * KVH * HD
    grouped = HQ // KVH
    span_keys = TOPP * PLEN + QLEN
    scale = 1.0 / HD**0.5
    row_count = requests * RECOMP
    hidden = recomp_hidden.reshape(row_count, D).astype(jnp.float32)
    normed = (
        hidden * lax.rsqrt(jnp.mean(hidden * hidden, axis=1, keepdims=True) + EPSILON)
    ).astype(jnp.bfloat16)
    head_columns = lax.all_gather(w_kv, "group", axis=1, tiled=True)
    projected = jnp.dot(
        normed,
        lax.all_gather(head_columns, "member", axis=0, tiled=True),
        preferred_element_type=jnp.float32,
    )
    recomputed = projected.astype(jnp.bfloat16).reshape(requests, RECOMP, kv_width)
    wanted = retrieval.reshape(requests)
    pass_local = cache.shape[0]
    holders_count = lax.axis_size("member")
    my_index = lax.axis_index("member")
    capacity = -(-requests // holders_count)
    request_table = lax.all_gather(wanted.reshape(1, requests), "member", axis=0, tiled=True)
    mine_mask = request_table // pass_local == my_index
    earlier_mask = (jnp.arange(requests)[:, None] < jnp.arange(requests)[None, :]).astype(jnp.int32)
    slot_rank = jnp.dot(mine_mask.astype(jnp.int32), earlier_mask)
    slot_table = mine_mask[:, None, :] & (
        slot_rank[:, None, :] == jnp.arange(capacity)[None, :, None]
    )
    local_index = jnp.sum(
        jnp.where(slot_table, (request_table % pass_local)[:, None, :], 0), axis=2
    )
    slot_filled = jnp.any(slot_table, axis=2)
    outgoing = jnp.where(
        slot_filled[:, :, None, None], cache[local_index], jnp.zeros((), cache.dtype)
    )
    arrived = lax.all_to_all(outgoing, "member", split_axis=0, concat_axis=0, tiled=True)
    holder_of = wanted // pass_local
    same_holder = holder_of[:, None] == holder_of[None, :]
    before_me = jnp.arange(requests)[None, :] < jnp.arange(requests)[:, None]
    copy_rank = jnp.sum((same_holder & before_me).astype(jnp.int32), axis=1)
    blocks = arrived.reshape(holders_count * capacity, PLEN, kv_width)[
        holder_of * capacity + copy_rank
    ]
    spots = positions.reshape(requests, RECOMP)
    onehot = spots[:, :, None] == jnp.arange(PLEN)[None, None, :]
    covered = jnp.any(onehot, axis=1)
    placed = jnp.einsum(
        "krp,kre->kpe", onehot.astype(jnp.bfloat16), recomputed, preferred_element_type=jnp.float32
    ).astype(jnp.bfloat16)
    context = jnp.where(covered[:, :, None], placed, blocks).reshape(
        query_count, TOPP * PLEN, kv_width
    )
    context = jnp.concatenate([context, own_kv.reshape(query_count, QLEN, kv_width)], axis=1)
    keys = context[:, :, : KVH * HD].reshape(query_count, span_keys, KVH, HD)
    values = context[:, :, KVH * HD :].reshape(query_count, span_keys, KVH, HD)
    queries = q_rows.reshape(query_count, QLEN, KVH, grouped, HD)
    token_pos = jnp.arange(QLEN)[:, None]
    key_pos = jnp.arange(span_keys)[None, :]
    visible = (key_pos < TOPP * PLEN) | (key_pos - TOPP * PLEN <= token_pos)

    def attend(operands):
        query_block, key_block, value_block = operands
        scores = (
            jnp.einsum("tkgd,skd->kgts", query_block, key_block, preferred_element_type=jnp.float32)
            * scale
        )
        scores = jnp.where(visible, scores, -jnp.inf)
        peak = jnp.max(scores, axis=-1, keepdims=True)
        expd = jnp.exp(scores - peak)
        probs = (expd / jnp.sum(expd, axis=-1, keepdims=True)).astype(jnp.bfloat16)
        output = jnp.einsum(
            "kgts,skd->tkgd", probs, value_block, preferred_element_type=jnp.float32
        )
        return output.astype(jnp.bfloat16).reshape(QLEN, HQ * HD)

    results = lax.map(attend, (queries, keys, values))
    return results.reshape(query_count * QLEN, HQ * HD)


def solution(mesh):
    placed = (
        P(("group", "member"), None),
        P(("group", "member"), None),
        P(("group", "member"), None, None),
        P(("group", "member"), None, None, None),
        P("member", "group"),
        P(("group", "member"), None),
        P(("group", "member"), None, None),
    )
    return jax.shard_map(
        local, mesh=mesh, in_specs=placed, out_specs=P(("group", "member"), None), check_vma=False
    )
```

profile of v0, /device:TPU:32, one launch (start us, length us, event | category | flops | bytes accessed | tf_op | source)
XLA Modules:
  0.0 287.2 jit_solution(2852515802772880683)
XLA Ops:
  6.5 0.0 copy-start
  6.5 0.0 all-gather.3.cloned.1.call-start
  6.5 13.6 %all_gather.9 = bf16[128,1024]{1,0:T(8,128)(2,1)} all-gather(bf16[128,128]{1,0:T(8,128)(2,1)} %param.13), channel_id=1, replica_groups=mesh['group'=8,'member'=32] {'group'}, dimensions={1}, use_global_device_ids=true | all-gather | bytes 294912 | tf_op jit(solution)/shard_map/all_gather | solution.py:29
  20.2 0.0 all-gather.3.cloned.1.call-update
  20.2 0.8 reshape.252
  21.0 40.2 %all-gather = s32[32,1,16]{2,1,0:T(1,128)S(1)} all-gather(s32[1,1,16]{2,1,0:T(1,128)S(1)} %reshape.252), channel_id=1, replica_groups=mesh['group'=8,'member'=32] {'member'}, dimensions={0}, use_global_device_ids=true | all-gather | bytes 2112 | tf_op jit(solution)/shard_map/all_gather | solution.py:41
  61.2 0.1 copy.33
  61.3 0.2 fusion.37
  61.5 0.0 copy-done
  61.5 2.8 gather_fusion
  64.4 4.5 %bitcast_select_fusion.4 = bf16[32,1,64,1024]{3,2,1,0:T(8,128)(2,1)} fusion(bf16[32,64,1024]{2,1,0:T(8,128)(2,1)} %gather_fusion, pred[32]{0:T(512)(128)(4,1)S(1)} %reduce_or.19), kind=kLoop, calls=%fused_computation.31 | loop fusion | flops 2097152 | bytes 8388640 | tf_op jit(solution)/shard_map/jit(_where)/select_n | solution.py:52
  68.9 0.0 copy-start.5
  68.9 8.1 %all-to-all-start = ((bf16[32,1,64,1024]{3,2,1,0:T(8,128)(2,1)}), bf16[32,1,64,1024]{3,2,1,0:T(8,128)(2,1)}, u32[]{:S(2)}, u32[]{:S(2)}) async-start(bf16[32,1,64,1024]{3,2,1,0:T(8,128)(2,1)} %bitcast_select_fusion.4), calls=%async_computation | async-start | bytes 8388608 | tf_op jit(solution)/shard_map/all_to_all | solution.py:55
  77.0 0.0 copy-done.5
  77.0 0.1 reshape.228
  77.1 0.1 reshape.227
  77.2 0.0 copy-done.2
  77.2 0.5 multiply_reduce_fusion
  77.7 0.1 rsqrt.12
  77.8 0.0 copy-done.3
  77.8 0.3 copy.35
  78.0 0.0 copy-start.4
  78.1 5.4 %copy.46 = bf16[32,8,64,128]{3,2,1,0:T(8,128)(2,1)} copy(bf16[32,8,64,128]{3,1,2,0:T(8,128)(2,1)} %bitcast.134) | data formatting | bytes 8388608
  83.4 0.2 convert_reduce_fusion
  83.7 0.0 copy-done.4
  83.7 0.1 fusion.33
  83.8 1.9 fusion.30
  85.7 118.0 %all-to-all-done = bf16[32,1,64,1024]{3,2,1,0:T(8,128)(2,1)} async-done(((bf16[32,1,64,1024]{3,2,1,0:T(8,128)(2,1)}), bf16[32,1,64,1024]{3,2,1,0:T(8,128)(2,1)}, u32[]{:S(2)}, u32[]{:S(2)}) %all-to-all-start) | async-done | bytes 4194336 | tf_op jit(solution)/shard_map/all_to_all | solution.py:55
  203.7 2.9 gather_fusion.1
  206.6 0.0 all-gather.3.cloned.1.call-done
  206.6 6.3 %convolution_convert_fusion = bf16[256,1024]{1,0:T(8,128)(2,1)S(1)} fusion(bf16[256,4096]{1,0:T(8,128)(2,1)} %fusion.30, bf16[4096,1024]{1,0:T(8,128)(2,1)} %all-gather.3.cloned.1.call-done), kind=kOutput, calls=%fused_computation.40 | convolution fusion | flops 2147745792 | bytes 11010048 | tf_op jit(solution)/shard_map/dot_general | solution.py:30
  213.0 2.6 convert_select_fusion
  215.6 2.9 copy.34
  218.4 1.7 pad_maximum_fusion
  220.2 59.2 %while.11 = (s32[]{:T(128)}, bf16[2,128,8192]{2,1,0:T(8,128)(2,1)}, bf16[2,640,4,128]{1,3,2,0:T(8,128)(2,1)}, bf16[2,640,4,128]{1,3,2,0:T(8,128)(2,1)}, bf16[2,1...) while((s32[]{:T(128)}, bf16[2,128,8192]{2,1,0:T(8,128)(2,1)}, ...), condition=%wide.region_8.9_spmd.clone, body=%wide.region_5.8_spmd.clone.sunk | while | flops 2717024768 | bytes 60265176 | solution.py:95
  220.2 2.0 constant_dynamic-slice_fusion.2
  222.2 0.2 fusion.72
  222.4 12.5 %fusion.73 = (f32[4,16,128]{2,1,0:T(8,128)S(1)}, f32[4,16,128,640]{2,3,1,0:T(8,128)}) fusion(pred[128,640]{0,1:T(8,128)(4,1)S(1)} %fusion.72, bf16[1,128,4,16,128]{4,3,2,1,0:T(8,128)(2,1)S(1)} %constant_dynamic-slice_fusion.2, bf16[2,640,4,128]{1,3,2,0:T(8,128)(2,1)} %get-tuple-element.170, s32[]{:T(128)} %get-tuple-element.159), kind=kOutput, calls=%fused_computation.92.clone.1 | convolution fusion | flops 1363149440 | bytes 23839232 | tf_op jit(solution)/shard_map/while/body/eval_jaxpr/sub | solution.py:88
  234.9 10.4 %fusion.74 = bf16[4,128,16,128]{3,1,2,0:T(8,128)(2,1)} fusion(f32[4,16,128,640]{2,3,1,0:T(8,128)} %get-tuple-element.149, f32[4,16,128]{2,1,0:T(8,128)S(1)} %get-tuple-element.150, bf16[2,640,4,128]{1,3,2,0:T(8,128)(2,1)} %get-tuple-element.169, s32[]{:T(128)} %get-tuple-element.159), kind=kOutput, calls=%fused_computation.14.clone.1 | convolution fusion | flops 1353711616 | bytes 23757312 | tf_op jit(solution)/shard_map/while/body/eval_jaxpr/kgts,skd->tkgd/dot_general | solution.py:90
  245.4 2.9 %copy.61 = bf16[1,128,8192]{2,1,0:T(8,128)(2,1)S(1)} copy(bf16[1,128,8192]{1,2,0:T(8,128)(2,1)} %bitcast.131) | data formatting | bytes 4194304 | tf_op jit(solution)/shard_map/while/body/jit(dynamic_update_index_in_dim)/dynamic_update_slice | solution.py:95
  248.3 1.5 constant_dynamic-update-slice_fusion.2
  249.8 2.0 constant_dynamic-slice_fusion.2
  251.8 0.2 fusion.72
  252.0 12.5 %fusion.73 = (f32[4,16,128]{2,1,0:T(8,128)S(1)}, f32[4,16,128,640]{2,3,1,0:T(8,128)}) fusion(pred[128,640]{0,1:T(8,128)(4,1)S(1)} %fusion.72, bf16[1,128,4,16,128]{4,3,2,1,0:T(8,128)(2,1)S(1)} %constant_dynamic-slice_fusion.2, bf16[2,640,4,128]{1,3,2,0:T(8,128)(2,1)} %get-tuple-element.170, s32[]{:T(128)} %get-tuple-element.159), kind=kOutput, calls=%fused_computation.92.clone.1 | convolution fusion | flops 1363149440 | bytes 23839232 | tf_op jit(solution)/shard_map/while/body/eval_jaxpr/sub | solution.py:88
  264.5 10.4 %fusion.74 = bf16[4,128,16,128]{3,1,2,0:T(8,128)(2,1)} fusion(f32[4,16,128,640]{2,3,1,0:T(8,128)} %get-tuple-element.149, f32[4,16,128]{2,1,0:T(8,128)S(1)} %get-tuple-element.150, bf16[2,640,4,128]{1,3,2,0:T(8,128)(2,1)} %get-tuple-element.169, s32[]{:T(128)} %get-tuple-element.159), kind=kOutput, calls=%fused_computation.14.clone.1 | convolution fusion | flops 1353711616 | bytes 23757312 | tf_op jit(solution)/shard_map/while/body/eval_jaxpr/kgts,skd->tkgd/dot_general | solution.py:90
  275.0 2.9 %copy.61 = bf16[1,128,8192]{2,1,0:T(8,128)(2,1)S(1)} copy(bf16[1,128,8192]{1,2,0:T(8,128)(2,1)} %bitcast.131) | data formatting | bytes 4194304 | tf_op jit(solution)/shard_map/while/body/jit(dynamic_update_index_in_dim)/dynamic_update_slice | solution.py:95
  277.9 1.5 constant_dynamic-update-slice_fusion.2
  279.4 1.0 copy-done.1
  (13 shorter events, 0.1 us)
Async XLA Ops:
  6.5 55.0 %copy-start = (bf16[4,64,1024]{2,1,0:T(8,128)(2,1)S(1)}, bf16[4,64,1024]{2,1,0:T(8,128)(2,1)}, u32[]{:S(2)}) copy-start(bf16[4,64,1024]{2,1,0:T(8,128)(2,1)} %param.11) | copy-start | bytes 1572868
  6.5 200.1 %all-gather.3.cloned.1.call-start = ((), (), s32[]{:S(2)}) async-start(), calls=%async_computation.1 | async-start | bytes 8650752 | tf_op jit(solution)/shard_map/all_gather | solution.py:32
  68.9 8.1 %copy-start.5 = (s32[2,8]{1,0:T(2,128)S(1)}, s32[2,8]{1,0:T(2,128)}, u32[]{:S(2)}) copy-start(s32[2,8]{1,0:T(2,128)} %param.14) | copy-start | bytes 196
  68.9 8.3 %copy-start.2 = (bf16[2,8,16,4096]{3,2,1,0:T(8,128)(2,1)S(1)}, bf16[2,8,16,4096]{3,2,1,0:T(8,128)(2,1)}, u32[]{:S(2)}) copy-start(bf16[2,8,16,4096]{3,2,1,0:T(8,128)(2,1)} %param.12) | copy-start | bytes 6291460
  68.9 8.9 %copy-start.3 = (bf16[256,1024]{1,0:T(8,128)(2,1)S(1)}, bf16[256,1024]{1,0:T(8,128)(2,1)}, u32[]{:S(2)}) copy-start(bf16[256,1024]{1,0:T(8,128)(2,1)} %param.10) | copy-start | bytes 1572868
  68.9 134.8 %all-to-all-start = ((bf16[32,1,64,1024]{3,2,1,0:T(8,128)(2,1)}), bf16[32,1,64,1024]{3,2,1,0:T(8,128)(2,1)}, u32[]{:S(2)}, u32[]{:S(2)}) async-start(bf16[32,1,64,1024]{3,2,1,0:T(8,128)(2,1)} %bitcast_select_fusion.4), calls=%async_computation | async-start | bytes 8388608 | tf_op jit(solution)/shard_map/all_to_all | solution.py:55
  78.0 5.6 %copy-start.4 = (s32[2,8,16]{2,1,0:T(8,128)S(1)}, s32[2,8,16]{2,1,0:T(8,128)}, u32[]{:S(2)}) copy-start(s32[2,8,16]{2,1,0:T(8,128)} %param.15) | copy-start | bytes 3076
  279.4 1.0 copy-start.1
Sparse Core Ops, SparseCore 0:
  20.3 181.5 all-gather.2
where the time goes:
time: 288 us; the launch traced here: 287 us
  waiting for transfers between devices  118 us (41%)
  matrix products  55.1 us (19%)
  blocking collectives  53.9 us (19%)
  local copies, waits for them, and re-layouts  29.1 us (10%)
  between operations  13.5 us (5%)
  other arithmetic  9.49 us (3%)
  starting transfers between devices  8.12 us (3%)
    all_to_all x1, waiting for transfers between devices, local(): lax.all_to_all(outgoing, 'member', split_axis=0, concat_axis=0, tiled=True)  118 us
    all_gather x1, blocking collectives, local(): lax.all_gather(wanted.reshape(1, requests), 'member', axis=0, tiled=True)  40.2 us
    sub x2, matrix products, attend(): expd = jnp.exp(scores - peak)  25.1 us
    dot_general x2, matrix products, attend(): jnp.einsum('kgts,skd->tkgd', probs, value_block, preferred_element_type=j...  20.9 us
    all_gather x1, blocking collectives, local(): head_columns = lax.all_gather(w_kv, 'group', axis=1, tiled=True)  13.6 us
    dynamic_update_slice x4, local copies, waits for them, and re-layouts, local(): results = lax.map(attend, (queries, keys, values))  8.71 us
    all_to_all x1, starting transfers between devices, local(): lax.all_to_all(outgoing, 'member', split_axis=0, concat_axis=0, tiled=True)  8.12 us
    unnamed x14, local copies, waits for them, and re-layouts  7.19 us
  transfers between devices with their start and end apart: 2, of which 1 were waited for; matrix products, arithmetic and copies ran while one was open for 7% of the time, Pallas kernels for 0%

commit v1 on v0

--- a/solution.py
+++ b/solution.py
@@ -38,7 +38,12 @@
     holders_count = lax.axis_size("member")
     my_index = lax.axis_index("member")
     capacity = -(-requests // holders_count)
-    request_table = lax.all_gather(wanted.reshape(1, requests), "member", axis=0, tiled=True)
+    request_table = jnp.concatenate(
+        lax.all_to_all(
+            jnp.stack([wanted.reshape(1, requests)] * lax.axis_size("member")), "member", 0, 0
+        ),
+        axis=0,
+    )
     mine_mask = request_table // pass_local == my_index
     earlier_mask = (jnp.arange(requests)[:, None] < jnp.arange(requests)[None, :]).astype(jnp.int32)
     slot_rank = jnp.dot(mine_mask.astype(jnp.int32), earlier_mask)

time: 288 us -> 272 us (0.944)
  blocking collectives: 53.9 us -> 13.6 us
  waiting for transfers between devices: 118 us -> 131 us
  starting transfers between devices: 8.12 us -> 17.5 us
    all_gather x1 -> x0, blocking collectives: 40.2 us -> none  [local(): lax.all_gather(wanted.reshape(1, requests), 'member', axis=0, tiled=True)]
    all_to_all x0 -> x1, starting transfers between devices: none -> 11.4 us  [local(): lax.all_to_all(jnp.stack([wanted.reshape(1, requests)] * lax.axis_size('m...]
    all_to_all x0 -> x1, waiting for transfers between devices: none -> 8.6 us  [local(): lax.all_to_all(jnp.stack([wanted.reshape(1, requests)] * lax.axis_size('m...]
    all_to_all x1, waiting for transfers between devices: 118 us -> 123 us  [local(): lax.all_to_all(outgoing, 'member', split_axis=0, concat_axis=0, tiled=True)]
    unnamed x14 -> x13, local copies, waits for them, and re-layouts: 7.19 us -> 6.43 us
  transfers between devices with their start and end apart: 2 -> 3, of which waited for: 1 -> 2; matrix products, arithmetic and copies ran while one was open for 7% -> 8% of each run, Pallas kernels for 0% -> 0%
where the time goes in v1:
time: 272 us; the launch traced here: 270 us
  waiting for transfers between devices  131 us (48%)
  matrix products  55.1 us (20%)
  local copies, waits for them, and re-layouts  29.6 us (11%)
  starting transfers between devices  17.5 us (6%)
  blocking collectives  13.6 us (5%)
  between operations  13.5 us (5%)
  other arithmetic  9.49 us (3%)
    all_to_all x1, waiting for transfers between devices, local(): lax.all_to_all(outgoing, 'member', split_axis=0, concat_axis=0, tiled=True)  123 us
    sub x2, matrix products, attend(): expd = jnp.exp(scores - peak)  25.1 us
    dot_general x2, matrix products, attend(): jnp.einsum('kgts,skd->tkgd', probs, value_block, preferred_element_type=j...  20.9 us
    all_gather x1, blocking collectives, local(): head_columns = lax.all_gather(w_kv, 'group', axis=1, tiled=True)  13.6 us
    all_to_all x1, starting transfers between devices, local(): lax.all_to_all(jnp.stack([wanted.reshape(1, requests)] * lax.axis_size('m...  11.4 us
    dynamic_update_slice x4, local copies, waits for them, and re-layouts, local(): results = lax.map(attend, (queries, keys, values))  8.71 us
    all_to_all x1, waiting for transfers between devices, local(): lax.all_to_all(jnp.stack([wanted.reshape(1, requests)] * lax.axis_size('m...  8.6 us
    unnamed x13, local copies, waits for them, and re-layouts  6.43 us
  transfers between devices with their start and end apart: 3, of which 2 were waited for; matrix products, arithmetic and copies ran while one was open for 8% of the time, Pallas kernels for 0%

profile of v1, /device:TPU:32, one launch (start us, length us, event | category | flops | bytes accessed | tf_op | source)
XLA Modules:
  0.0 270.3 jit_solution(10718499953830397325)
XLA Ops:
  6.5 0.0 copy-start
  6.5 0.0 all-gather.2.cloned.1.call-start
  6.5 13.6 %all_gather.6 = bf16[128,1024]{1,0:T(8,128)(2,1)} all-gather(bf16[128,128]{1,0:T(8,128)(2,1)} %param.13), channel_id=1, replica_groups=mesh['group'=8,'member'=32] {'group'}, dimensions={1}, use_global_device_ids=true | all-gather | bytes 294912 | tf_op jit(solution)/shard_map/all_gather | solution.py:29
  20.2 0.0 all-gather.2.cloned.1.call-update
  20.2 0.8 stack_reshape_reshape.2
  21.0 0.6 stack.3
  21.6 11.4 %all-to-all-start = ((s32[32,1,16]{2,1,0:T(1,128)}), s32[32,1,16]{2,1,0:T(1,128)S(1)}, u32[]{:S(2)}, u32[]{:S(2)}) async-start(s32[32,1,16]{2,1,0:T(1,128)} %stack.3), calls=%async_computation | async-start | bytes 32768 | tf_op jit(solution)/shard_map/all_to_all | solution.py:42
  33.0 8.6 %all-to-all-done = s32[32,1,16]{2,1,0:T(1,128)S(1)} async-done(((s32[32,1,16]{2,1,0:T(1,128)}), s32[32,1,16]{2,1,0:T(1,128)S(1)}, u32[]{:S(2)}, u32[]{:S(2)}) %all-to-all-start) | async-done | bytes 2080 | tf_op jit(solution)/shard_map/all_to_all | solution.py:42
  41.6 0.1 copy.30
  41.6 0.2 fusion.37
  41.9 0.0 copy-done
  41.9 2.8 %gather_fusion = bf16[32,64,1024]{2,1,0:T(8,128)(2,1)} fusion(bf16[4,64,1024]{2,1,0:T(8,128)(2,1)S(1)} %copy-done, s32[1024]{0:T(1024)S(1)} %pad_clamp_fusion.1), kind=kCustom, calls=%fused_computation | custom fusion | bytes 8388736 | tf_op jit(solution)/shard_map/gather | solution.py:58
  44.7 4.5 %bitcast_select_fusion.4 = bf16[32,1,64,1024]{3,2,1,0:T(8,128)(2,1)} fusion(bf16[32,64,1024]{2,1,0:T(8,128)(2,1)} %gather_fusion, pred[32]{0:T(512)(128)(4,1)S(1)} %reduce_or.19), kind=kLoop, calls=%fused_computation.31 | loop fusion | flops 2097152 | bytes 8388640 | tf_op jit(solution)/shard_map/jit(_where)/select_n | solution.py:57
  49.2 6.1 %all-to-all-start.1 = ((bf16[32,1,64,1024]{3,2,1,0:T(8,128)(2,1)}), bf16[32,1,64,1024]{3,2,1,0:T(8,128)(2,1)}, u32[]{:S(2)}, u32[]{:S(2)}) async-start(bf16[32,1,64,1024]{3,2,1,0:T(8,128)(2,1)} %bitcast_select_fusion.4), calls=%async_computation.1 | async-start | bytes 8388608 | tf_op jit(solution)/shard_map/all_to_all | solution.py:60
  55.3 0.0 copy-done.5
  55.3 0.1 reshape.233
  55.4 0.0 copy-done.2
  55.4 0.5 multiply_reduce_fusion
  55.9 0.1 rsqrt.12
  56.0 0.0 copy-done.3
  56.0 0.3 copy.32
  56.3 0.0 copy-start.4
  56.3 5.4 %copy.43 = bf16[32,8,64,128]{3,2,1,0:T(8,128)(2,1)} copy(bf16[32,8,64,128]{3,1,2,0:T(8,128)(2,1)} %bitcast.134) | data formatting | bytes 8388608
  61.7 0.2 convert_reduce_fusion
  61.9 0.0 copy-done.4
  61.9 0.1 fusion.33
  62.0 1.9 fusion.30
  64.0 122.8 %all-to-all-done.1 = bf16[32,1,64,1024]{3,2,1,0:T(8,128)(2,1)} async-done(((bf16[32,1,64,1024]{3,2,1,0:T(8,128)(2,1)}), bf16[32,1,64,1024]{3,2,1,0:T(8,128)(2,1)}, u32[]{:S(2)}, u32[]{:S(2)}) %all-to-all-start.1) | async-done | bytes 4194336 | tf_op jit(solution)/shard_map/all_to_all | solution.py:60
  186.8 2.9 %gather_fusion.1 = bf16[16,64,1024]{2,1,0:T(8,128)(2,1)S(1)} fusion(bf16[32,64,1024]{2,1,0:T(8,128)(2,1)} %bitcast.7, s32[1024]{0:T(1024)S(1)} %pad_clamp_fusion), kind=kCustom, calls=%fused_computation.1 | custom fusion | bytes 4194368 | tf_op jit(solution)/shard_map/gather | solution.py:65
  189.7 0.0 all-gather.2.cloned.1.call-done
  189.7 6.3 %convolution_convert_fusion = bf16[256,1024]{1,0:T(8,128)(2,1)S(1)} fusion(bf16[256,4096]{1,0:T(8,128)(2,1)} %fusion.30, bf16[4096,1024]{1,0:T(8,128)(2,1)} %all-gather.2.cloned.1.call-done), kind=kOutput, calls=%fused_computation.40 | convolution fusion | flops 2147745792 | bytes 11010048 | tf_op jit(solution)/shard_map/dot_general | solution.py:30
  196.1 2.6 convert_select_fusion
  198.6 2.9 %copy.31 = bf16[2,512,1024]{1,2,0:T(8,128)(2,1)S(1)} copy(bf16[2,512,1024]{2,1,0:T(8,128)(2,1)} %bitcast.133) | data formatting | bytes 4194304 | tf_op jit(solution)/shard_map/reshape | solution.py:74
  201.5 1.7 pad_maximum_fusion
  203.2 59.2 %while.11 = (s32[]{:T(128)}, bf16[2,128,8192]{2,1,0:T(8,128)(2,1)}, bf16[2,640,4,128]{1,3,2,0:T(8,128)(2,1)}, bf16[2,640,4,128]{1,3,2,0:T(8,128)(2,1)}, bf16[2,1...) while((s32[]{:T(128)}, bf16[2,128,8192]{2,1,0:T(8,128)(2,1)}, ...), condition=%wide.region_8.9_spmd.clone, body=%wide.region_5.8_spmd.clone.sunk | while | flops 2717024768 | bytes 60265176 | solution.py:100
  203.2 2.0 constant_dynamic-slice_fusion.2
  205.3 0.2 fusion.72
  205.5 12.5 %fusion.73 = (f32[4,16,128]{2,1,0:T(8,128)S(1)}, f32[4,16,128,640]{2,3,1,0:T(8,128)}) fusion(pred[128,640]{0,1:T(8,128)(4,1)S(1)} %fusion.72, bf16[1,128,4,16,128]{4,3,2,1,0:T(8,128)(2,1)S(1)} %constant_dynamic-slice_fusion.2, bf16[2,640,4,128]{1,3,2,0:T(8,128)(2,1)} %get-tuple-element.170, s32[]{:T(128)} %get-tuple-element.159), kind=kOutput, calls=%fused_computation.92.clone.1 | convolution fusion | flops 1363149440 | bytes 23839232 | tf_op jit(solution)/shard_map/while/body/eval_jaxpr/sub | solution.py:93
  218.0 10.4 %fusion.74 = bf16[4,128,16,128]{3,1,2,0:T(8,128)(2,1)} fusion(f32[4,16,128,640]{2,3,1,0:T(8,128)} %get-tuple-element.149, f32[4,16,128]{2,1,0:T(8,128)S(1)} %get-tuple-element.150, bf16[2,640,4,128]{1,3,2,0:T(8,128)(2,1)} %get-tuple-element.169, s32[]{:T(128)} %get-tuple-element.159), kind=kOutput, calls=%fused_computation.14.clone.1 | convolution fusion | flops 1353711616 | bytes 23757312 | tf_op jit(solution)/shard_map/while/body/eval_jaxpr/kgts,skd->tkgd/dot_general | solution.py:95
  228.5 2.9 %copy.58 = bf16[1,128,8192]{2,1,0:T(8,128)(2,1)S(1)} copy(bf16[1,128,8192]{1,2,0:T(8,128)(2,1)} %bitcast.131) | data formatting | bytes 4194304 | tf_op jit(solution)/shard_map/while/body/jit(dynamic_update_index_in_dim)/dynamic_update_slice | solution.py:100
  231.4 1.5 constant_dynamic-update-slice_fusion.2
  232.8 2.0 constant_dynamic-slice_fusion.2
  234.9 0.2 fusion.72
  235.1 12.5 %fusion.73 = (f32[4,16,128]{2,1,0:T(8,128)S(1)}, f32[4,16,128,640]{2,3,1,0:T(8,128)}) fusion(pred[128,640]{0,1:T(8,128)(4,1)S(1)} %fusion.72, bf16[1,128,4,16,128]{4,3,2,1,0:T(8,128)(2,1)S(1)} %constant_dynamic-slice_fusion.2, bf16[2,640,4,128]{1,3,2,0:T(8,128)(2,1)} %get-tuple-element.170, s32[]{:T(128)} %get-tuple-element.159), kind=kOutput, calls=%fused_computation.92.clone.1 | convolution fusion | flops 1363149440 | bytes 23839232 | tf_op jit(solution)/shard_map/while/body/eval_jaxpr/sub | solution.py:93
  247.6 10.4 %fusion.74 = bf16[4,128,16,128]{3,1,2,0:T(8,128)(2,1)} fusion(f32[4,16,128,640]{2,3,1,0:T(8,128)} %get-tuple-element.149, f32[4,16,128]{2,1,0:T(8,128)S(1)} %get-tuple-element.150, bf16[2,640,4,128]{1,3,2,0:T(8,128)(2,1)} %get-tuple-element.169, s32[]{:T(128)} %get-tuple-element.159), kind=kOutput, calls=%fused_computation.14.clone.1 | convolution fusion | flops 1353711616 | bytes 23757312 | tf_op jit(solution)/shard_map/while/body/eval_jaxpr/kgts,skd->tkgd/dot_general | solution.py:95
  258.1 2.9 %copy.58 = bf16[1,128,8192]{2,1,0:T(8,128)(2,1)S(1)} copy(bf16[1,128,8192]{1,2,0:T(8,128)(2,1)} %bitcast.131) | data formatting | bytes 4194304 | tf_op jit(solution)/shard_map/while/body/jit(dynamic_update_index_in_dim)/dynamic_update_slice | solution.py:100
  261.0 1.5 constant_dynamic-update-slice_fusion.2
  262.4 1.0 copy-done.1
  (14 shorter events, 0.1 us)
Async XLA Ops:
  6.5 35.3 %copy-start = (bf16[4,64,1024]{2,1,0:T(8,128)(2,1)S(1)}, bf16[4,64,1024]{2,1,0:T(8,128)(2,1)}, u32[]{:S(2)}) copy-start(bf16[4,64,1024]{2,1,0:T(8,128)(2,1)} %param.11) | copy-start | bytes 1572868
  6.5 183.2 %all-gather.2.cloned.1.call-start = ((), (), s32[]{:S(2)}) async-start(), calls=%async_computation.2 | async-start | bytes 8650752 | tf_op jit(solution)/shard_map/all_gather | solution.py:32
  21.6 20.0 %all-to-all-start = ((s32[32,1,16]{2,1,0:T(1,128)}), s32[32,1,16]{2,1,0:T(1,128)S(1)}, u32[]{:S(2)}, u32[]{:S(2)}) async-start(s32[32,1,16]{2,1,0:T(1,128)} %stack.3), calls=%async_computation | async-start | bytes 32768 | tf_op jit(solution)/shard_map/all_to_all | solution.py:42
  49.2 6.1 %copy-start.5 = (s32[2,8]{1,0:T(2,128)S(1)}, s32[2,8]{1,0:T(2,128)}, u32[]{:S(2)}) copy-start(s32[2,8]{1,0:T(2,128)} %param.14) | copy-start | bytes 196
  49.2 6.2 %copy-start.2 = (bf16[2,8,16,4096]{3,2,1,0:T(8,128)(2,1)S(1)}, bf16[2,8,16,4096]{3,2,1,0:T(8,128)(2,1)}, u32[]{:S(2)}) copy-start(bf16[2,8,16,4096]{3,2,1,0:T(8,128)(2,1)} %param.12) | copy-start | bytes 6291460
  49.2 6.8 %copy-start.3 = (bf16[256,1024]{1,0:T(8,128)(2,1)S(1)}, bf16[256,1024]{1,0:T(8,128)(2,1)}, u32[]{:S(2)}) copy-start(bf16[256,1024]{1,0:T(8,128)(2,1)} %param.10) | copy-start | bytes 1572868
  49.2 137.6 %all-to-all-start.1 = ((bf16[32,1,64,1024]{3,2,1,0:T(8,128)(2,1)}), bf16[32,1,64,1024]{3,2,1,0:T(8,128)(2,1)}, u32[]{:S(2)}, u32[]{:S(2)}) async-start(bf16[32,1,64,1024]{3,2,1,0:T(8,128)(2,1)} %bitcast_select_fusion.4), calls=%async_computation.1 | async-start | bytes 8388608 | tf_op jit(solution)/shard_map/all_to_all | solution.py:60
  56.3 5.6 %copy-start.4 = (s32[2,8,16]{2,1,0:T(8,128)S(1)}, s32[2,8,16]{2,1,0:T(8,128)}, u32[]{:S(2)}) copy-start(s32[2,8,16]{2,1,0:T(8,128)} %param.15) | copy-start | bytes 3076
  262.4 1.0 copy-start.1
Sparse Core Ops, SparseCore 0:
  20.3 167.9 all-gather.1
